TPU v7x, 512 devices: a whole 4x4x16 slice. The times are simulated.
512 devices in a mesh: seq: 64 (over x, z), tp: 8 (over y, core).
Axes of the slice: x: 4, y: 4, z: 16, core: 2. Of those that a mesh axis runs over, the one named last changes fastest.
Arguments:
- queries: bfloat16 [4, 1024], P(None, 'tp'), may hold values from -6 to 6
- keys_new: bfloat16 [4, 1024], P(None, 'tp'), may hold values from -32 to 32
- values_new: bfloat16 [4, 1024], P(None, 'tp'), may hold values from -6 to 6
- key_cache: bfloat16 [4, 4096, 1024], P(None, 'seq', 'tp'), may hold values from -32 to 32
- value_cache: bfloat16 [4, 4096, 1024], P(None, 'seq', 'tp'), may hold values from -6 to 6
- buckets: int32 [4, 4096], P(None, 'seq'), may hold values from 0 to 31
- lengths: int32 [4], replicated, may hold values from 1 to 4096, as said below
- bias_table: float32 [32, 16], replicated, may hold values from -3 to 3
- out_proj: bfloat16 [1024, 1024], P('tp'), may hold values from -0.1875 to 0.1875
- decode_in: bfloat16 [4, 1024], replicated, may hold values from -6 to 6
- prefill_in: bfloat16 [32768, 1024], P(('seq', 'tp')), may hold values from -6 to 6
- routes: int32 [32768, 2], P(('seq', 'tp')), may hold values from 0 to 15, all different within a row; in each aligned block of 64 rows (0 to 63, 64 to 127, ...) at most 10 rows name the same one
- gates: float32 [32768, 2], P(('seq', 'tp')), may hold values from 0.2 to 1
- dec_routes: int32 [4, 2], replicated, may hold values from 0 to 15, as said below
- dec_gates: float32 [4, 2], replicated, may hold values from 0.2 to 1
- norm_gain: float32 [1024], replicated, may hold values from 0.1 to 1.9
- w_gate: bfloat16 [1024, 45056], P('tp', 'seq'), may hold values from -0.1875 to 0.1875
- w_up: bfloat16 [1024, 45056], P('tp', 'seq'), may hold values from -0.1875 to 0.1875
- w_down: bfloat16 [45056, 1024], P('seq', 'tp'), may hold values from -0.109375 to 0.109375
Outputs:
- decode_out: bfloat16 [4, 1024], replicated
- prefill_out: bfloat16 [32768, 1024], P(('seq', 'tp'))
Inputs may be any that keep to these rules, and one draw needn't show every extreme that they name: `routes`: in the 64 rows of one device no expert is named by more than 10 rows, a bound that some block reaches. `dec_routes`: the two experts of a decode token differ; some decode token names expert 0 and some names expert 16 - 1. `lengths`: some request has all 4096 positions and some has exactly 1.
All inputs are finite; a program needn't handle non-finite values.
Results may differ from a plain program's by a relative error of at most 0.0075.
Values may be sent and summed in bfloat16 or wider, within the bound.
A program may use at most 64 MiB of HBM per device.

v0:
```python
import math
import jax
import jax.numpy as jnp
from jax import lax
from jax.sharding import PartitionSpec as P

HD = 64
EXPERTS = 16
TOP = 2
CAP = 10


def combined_all(value, axis, join):
    pieces = jax.tree.map(lambda part: lax.all_gather(part, axis), value)
    head = jax.tree.map(lambda part: part[0], pieces)
    tail = jax.tree.map(lambda part: part[1:], pieces)
    so_far, _ = lax.scan(lambda so_far, section: (join(so_far, section), None), head, tail)
    return so_far


def rms_scale(hidden, norm_gain):
    values = hidden.astype(jnp.float32)
    meansq = jnp.mean(values * values, axis=-1, keepdims=True)
    return (values * lax.rsqrt(meansq + 1e-06) * norm_gain).astype(jnp.bfloat16)


def combine_parts(earlier, later):
    max_early, sum_early, acc_early = earlier
    max_late, sum_late, acc_late = later
    joint_max = jnp.maximum(max_early, max_late)
    scale_early = jnp.exp(max_early - joint_max)
    scale_late = jnp.exp(max_late - joint_max)
    joint_sum = sum_early * scale_early + sum_late * scale_late
    joint_acc = acc_early * scale_early[..., None] + acc_late * scale_late[..., None]
    return (joint_max, joint_sum, joint_acc)


def route_slots(route_rows, capacity):
    flat_routes = route_rows.reshape(-1)
    onehot = (flat_routes[:, None] == jnp.arange(EXPERTS, dtype=jnp.int32)[None, :]).astype(
        jnp.int32
    )
    earlier = jnp.cumsum(onehot, axis=0) - onehot
    slot_rank = jnp.sum(earlier * onehot, axis=1)
    return flat_routes * capacity + slot_rank


def pack_rows(normed, route_rows, capacity, shards):
    flat_index = route_slots(route_rows, capacity)
    source = jnp.repeat(normed, TOP, axis=0)
    feature_width = normed.shape[1]
    packed = jnp.zeros((EXPERTS * capacity, feature_width), jnp.bfloat16).at[flat_index].set(source)
    packed = packed.reshape(EXPERTS, capacity, feature_width)
    return (jnp.repeat(packed, shards, axis=0), flat_index)


def expert_block(row_block, weights):
    gate_full, up_full, down_full = weights
    gate_pre = jnp.dot(row_block, gate_full, preferred_element_type=jnp.float32)
    up_pre = jnp.dot(row_block, up_full, preferred_element_type=jnp.float32)
    act = (jax.nn.gelu(gate_pre, approximate=True) * up_pre).astype(jnp.bfloat16)
    return jnp.dot(act, down_full, preferred_element_type=jnp.float32).astype(jnp.bfloat16)


def expert_apply(received, weights):
    peer_count, slot_count, feature_width = received.shape
    partial_value = expert_block(received.reshape(peer_count * slot_count, feature_width), weights)
    return partial_value.reshape(peer_count, slot_count, feature_width)


def unpack_rows(returned, flat_index, shards, residual, gate_rows):
    peer_count, slot_count, feature_width = returned.shape
    summed = returned.astype(jnp.float32).reshape(EXPERTS, shards, slot_count, feature_width)
    summed = jnp.sum(summed, axis=1).reshape(EXPERTS * slot_count, feature_width)
    picked = jnp.take(summed, flat_index, axis=0).reshape(-1, TOP, feature_width)
    combined = residual.astype(jnp.float32) + jnp.sum(gate_rows[..., None] * picked, axis=1)
    return combined.astype(jnp.bfloat16)


def body(
    queries,
    keys_new,
    values_new,
    key_cache,
    value_cache,
    buckets,
    lengths,
    bias_table,
    out_proj,
    decode_in,
    prefill_in,
    routes,
    gates,
    dec_routes,
    dec_gates,
    norm_gain,
    w_gate,
    w_up,
    w_down,
):
    seq_count = lax.axis_size("seq")
    seq_index = lax.axis_index("seq")
    tp_index = lax.axis_index("tp")
    shards = seq_count // EXPERTS
    weights = (
        lax.all_gather(w_gate, "tp", axis=0, tiled=True),
        lax.all_gather(w_up, "tp", axis=0, tiled=True),
        lax.all_gather(w_down, "tp", axis=1, tiled=True),
    )
    normed_pre = rms_scale(prefill_in, norm_gain)
    request_count, heads_width = queries.shape
    heads_here = heads_width // HD
    ctx_local = key_cache.shape[1]
    score_scale = 1.0 / math.sqrt(HD)
    query_rows = queries.reshape(request_count, heads_here, HD)
    key_rows = key_cache.reshape(request_count, ctx_local, heads_here, HD)
    value_rows = value_cache.reshape(request_count, ctx_local, heads_here, HD).astype(jnp.float32)
    bias_here = lax.dynamic_slice_in_dim(bias_table, tp_index * heads_here, heads_here, 1)
    bucket_hot = (
        buckets[..., None] == jnp.arange(bias_table.shape[0], dtype=jnp.int32)[None, None, :]
    ).astype(jnp.float32)
    bias_rows = jnp.einsum("rcn,nh->rhc", bucket_hot, bias_here, precision=lax.Precision.HIGHEST)
    cache_scores = (
        jnp.einsum("rhd,rchd->rhc", query_rows, key_rows, preferred_element_type=jnp.float32)
        * score_scale
        + bias_rows
    )
    positions = seq_index * ctx_local + jnp.arange(ctx_local, dtype=jnp.int32)
    valid_mask = (positions[None, :] < lengths[:, None])[:, None, :]
    cache_scores = jnp.where(valid_mask, cache_scores, -1e30)
    local_max = jnp.max(cache_scores, axis=-1)
    local_weights = jnp.where(valid_mask, jnp.exp(cache_scores - local_max[..., None]), 0.0)
    local_sum = jnp.sum(local_weights, axis=-1)
    local_acc = jnp.einsum(
        "rhc,rchd->rhd", local_weights, value_rows, precision=lax.Precision.HIGHEST
    )
    part_max, part_sum, part_acc = combined_all(
        (local_max, local_sum, local_acc), "seq", combine_parts
    )
    own_key = keys_new.reshape(request_count, heads_here, HD).astype(jnp.float32)
    own_value = values_new.reshape(request_count, heads_here, HD).astype(jnp.float32)
    own_score = (
        jnp.sum(query_rows.astype(jnp.float32) * own_key, axis=-1) * score_scale
        + bias_here[0][None, :]
    )
    row_peak = jnp.maximum(part_max, own_score)
    keep_scale = jnp.exp(part_max - row_peak)
    own_weight = jnp.exp(own_score - row_peak)
    weight_total = part_sum * keep_scale + own_weight
    weighted = part_acc * keep_scale[..., None] + own_weight[..., None] * own_value
    mixed_rows = (
        (weighted / weight_total[..., None])
        .astype(jnp.bfloat16)
        .reshape(request_count, heads_width)
    )
    head_terms = jnp.dot(mixed_rows, out_proj, preferred_element_type=jnp.float32)
    attended = lax.psum(head_terms, "tp")
    decode_hidden = (decode_in.astype(jnp.float32) + attended).astype(jnp.bfloat16)
    normed_dec = rms_scale(decode_hidden, norm_gain)
    my_expert = seq_index // shards
    dec_part = expert_block(normed_dec, weights).astype(jnp.float32)
    gate_here = jnp.sum(jnp.where(dec_routes == my_expert, dec_gates, 0.0), axis=1)
    dec_terms = lax.psum(gate_here[:, None] * dec_part, "seq")
    decode_out = (decode_hidden.astype(jnp.float32) + dec_terms).astype(jnp.bfloat16)
    send_all, index_all = pack_rows(normed_pre, routes, CAP, shards)
    back_all = lax.all_to_all(
        expert_apply(
            lax.all_to_all(send_all, "seq", split_axis=0, concat_axis=0, tiled=True), weights
        ),
        "seq",
        split_axis=0,
        concat_axis=0,
        tiled=True,
    )
    prefill_out = unpack_rows(back_all, index_all, shards, prefill_in, gates)
    return (decode_out, prefill_out)


def solution(mesh):
    placed = (
        P(None, "tp"),
        P(None, "tp"),
        P(None, "tp"),
        P(None, "seq", "tp"),
        P(None, "seq", "tp"),
        P(None, "seq"),
        P(),
        P(),
        P("tp", None),
        P(),
        P(("seq", "tp"), None),
        P(("seq", "tp"), None),
        P(("seq", "tp"), None),
        P(),
        P(),
        P(),
        P("tp", "seq"),
        P("tp", "seq"),
        P("seq", "tp"),
    )
    return jax.shard_map(
        body, mesh=mesh, in_specs=placed, out_specs=(P(), P(("seq", "tp"), None)), check_vma=False
    )
```

profile of v0, /device:TPU:8, one launch (start us, length us, event | category | flops | bytes accessed | tf_op | source)
XLA Modules:
  0.0 734.8 jit_solution(8691198079200414398)
XLA Ops:
  7.2 0.7 all-gather.9.cloned.1.call-update
  7.9 0.8 copy.57
  8.7 0.1 reshape.149
  8.8 0.7 broadcast_multiply_fusion
  9.6 0.1 mul.213
  9.7 1.0 fusion.17
  10.8 1.0 fusion.19
  11.8 0.1 broadcast_in_dim.66
  12.0 0.1 reshape.174
  12.2 0.2 reduce_window_sum.11
  12.3 0.2 select_reduce_fusion
  12.5 0.6 copy-done.17
  13.1 1.2 scatter_custom_fusion
  14.3 0.1 reshape.151
  14.5 1.6 broadcast_in_dim.67
  16.1 18.7 %all-to-all-start = ((bf16[64,10,1024]{2,1,0:T(8,128)(2,1)}), bf16[64,10,1024]{2,1,0:T(8,128)(2,1)S(1)}, u32[]{:S(2)}, u32[]{:S(2)}) async-start(bf16[64,10,1024]{2,1,0:T(8,128)(2,1)} %bitcast.19), calls=%async_computation | async-start | bytes 4194304 | tf_op jit(solution)/shard_map/all_to_all | solution.py:168
  34.9 0.7 all-gather.11.cloned.1.call-update
  35.6 0.7 all-gather.13.cloned.1.call-update
  36.3 0.1 copy.67
  36.7 0.7 constant_dynamic-slice_fusion.1
  37.5 0.1 fusion.66
  37.6 0.2 fusion.65
  37.8 0.2 fusion.64
  38.0 0.2 fusion.23
  38.2 162.8 %all-gather.2 = f32[256,2,64]{2,1,0:T(2,128)S(1)} all-gather(f32[4,2,64]{2,1,0:T(2,128)S(1)} %bitcast.70), channel_id=4, replica_groups=mesh['seq'=64,'tp'=8] {'seq'}, dimensions={0}, use_global_device_ids=true | all-gather | bytes 133120 | tf_op jit(solution)/shard_map/all_gather | solution.py:14
  201.2 80.8 %all-gather.4 = f32[64,4,2]{1,2,0:T(2,128)S(1)} all-gather(f32[1,4,2]{1,2,0:T(2,128)S(1)} %bitcast.72), channel_id=3, replica_groups=mesh['seq'=64,'tp'=8] {'seq'}, dimensions={0}, use_global_device_ids=true | all-gather | bytes 2080 | tf_op jit(solution)/shard_map/all_gather | solution.py:14
  282.0 88.0 %all-gather.3 = f32[64,4,2]{1,2,0:T(2,128)S(1)} all-gather(f32[1,4,2]{1,2,0:T(2,128)S(1)} %bitcast.71), channel_id=2, replica_groups=mesh['seq'=64,'tp'=8] {'seq'}, dimensions={0}, use_global_device_ids=true | all-gather | bytes 2080 | tf_op jit(solution)/shard_map/all_gather | solution.py:14
  370.0 1.3 reshape.153
  371.3 4.4 fusion.68
  375.8 6.6 convolution_convert_fusion
  382.4 1.6 reshape.154
  384.1 14.8 %all-to-all-start.1 = ((bf16[64,10,1024]{2,1,0:T(8,128)(2,1)}), bf16[64,10,1024]{2,1,0:T(8,128)(2,1)S(1)}, u32[]{:S(2)}, u32[]{:S(2)}) async-start(bf16[64,10,1024]{2,1,0:T(8,128)(2,1)} %reshape.154), calls=%async_computation.1 | async-start | bytes 4194304 | tf_op jit(solution)/shard_map/all_to_all | solution.py:166
  399.0 18.6 %while.14 = (s32[]{:T(128)}, f32[4,2]{0,1:T(2,128)S(1)}, f32[4,2]{0,1:T(2,128)S(1)}, f32[4,2,64]{2,1,0:T(2,128)S(1)}, f32[63,4,2]{1,2,0:T(2,128)S(1)}, /*index=5...) while((s32[]{:T(128)}, f32[4,2]{0,1:T(2,128)S(1)}, f32[4,2]{0,1:T(2,128)S(1)}, ...), condition=%wide.region_3.4_spmd, body=%wide.region_2.3_spmd.sunk | while | flops 1586 | bytes 6685 | solution.py:17
  417.6 0.1 reduce_sum.81
  418.1 0.1 slice_reduce_fusion
  418.6 0.1 copy.59
  418.9 0.1 fusion.67
  419.0 21.6 %psum.14 = f32[4,1024]{1,0:T(4,128)S(1)} all-reduce(f32[4,1024]{1,0:T(4,128)S(1)} %fusion.67), channel_id=1, replica_groups=mesh['seq'=64,'tp'=8] {'tp'}, use_global_device_ids=true, to_apply=%region_5.6 | all-reduce | flops 4096 | bytes 32768 | tf_op jit(solution)/shard_map/psum | solution.py:157
  440.7 0.1 fusion.27
  440.8 1.8 fusion.59
  442.6 2.7 fusion.13
  445.3 279.1 %psum.15 = f32[4,1024]{1,0:T(4,128)S(1)} all-reduce(f32[4,1024]{1,0:T(4,128)S(1)} %fusion.13), channel_id=1, replica_groups=mesh['seq'=64,'tp'=8] {'seq'}, use_global_device_ids=true, to_apply=%region_8.9 | all-reduce | flops 4096 | bytes 32768 | tf_op jit(solution)/shard_map/psum | solution.py:163
  724.5 0.6 fusion.30
  725.1 0.4 convert_reduce_fusion
  725.6 0.8 gather_fusion
  726.4 0.3 gather.7
  726.7 0.8 multiply_reduce_fusion
  727.6 0.7 fusion.20
  (336 shorter events, 20.2 us)
Async XLA Ops:
  7.2 411.7 %copy-start = (bf16[128,1024]{1,0:T(8,128)(2,1)S(1)}, bf16[128,1024]{1,0:T(8,128)(2,1)}, u32[]{:S(2)}) copy-start(bf16[128,1024]{1,0:T(8,128)(2,1)} %param.29) | copy-start | bytes 786436
  7.2 364.1 %all-gather.9.cloned.1.call-start = ((), (), s32[]{:S(2)}) async-start(), calls=%async_computation.2 | async-start | bytes 1622016 | tf_op jit(solution)/shard_map/all_gather | solution.py:106
  12.5 0.6 copy-start.17
  16.1 20.2 %copy-start.6 = (bf16[4,64,128]{2,1,0:T(8,128)(2,1)S(1)}, bf16[4,64,128]{2,1,0:T(8,128)(2,1)}, u32[]{:S(2)}) copy-start(bf16[4,64,128]{2,1,0:T(8,128)(2,1)} %param.24) | copy-start | bytes 196612
  16.1 20.4 %copy-start.11 = (bf16[4,128]{1,0:T(4,128)(2,1)S(1)}, bf16[4,128]{1,0:T(4,128)(2,1)}, u32[]{:S(2)}) copy-start(bf16[4,128]{1,0:T(4,128)(2,1)} %param.21) | copy-start | bytes 3076
  16.1 20.5 %copy-start.7 = (bf16[4,64,128]{2,1,0:T(8,128)(2,1)S(1)}, bf16[4,64,128]{2,1,0:T(8,128)(2,1)}, u32[]{:S(2)}) copy-start(bf16[4,64,128]{2,1,0:T(8,128)(2,1)} %param.25) | copy-start | bytes 196612
  16.1 21.3 %copy-start.20 = (s32[4]{0:T(128)S(1)}, s32[4]{0:T(128)}, u32[]{:S(2)}) copy-start(s32[4]{0:T(128)} %param.27) | copy-start | bytes 52
  16.1 21.5 %copy-start.19 = (s32[4,64]{1,0:T(4,128)S(1)}, s32[4,64]{1,0:T(4,128)}, u32[]{:S(2)}) copy-start(s32[4,64]{1,0:T(4,128)} %param.26) | copy-start | bytes 3076
  16.1 353.8 %all-to-all-start = ((bf16[64,10,1024]{2,1,0:T(8,128)(2,1)}), bf16[64,10,1024]{2,1,0:T(8,128)(2,1)S(1)}, u32[]{:S(2)}, u32[]{:S(2)}) async-start(bf16[64,10,1024]{2,1,0:T(8,128)(2,1)} %bitcast.19), calls=%async_computation | async-start | bytes 4194304 | tf_op jit(solution)/shard_map/all_to_all | solution.py:168
  34.8 340.9 %all-gather.11.cloned.1.call-start = ((), (), s32[]{:S(2)}) async-start(), calls=%async_computation.3 | async-start | bytes 1622016 | tf_op jit(solution)/shard_map/all_gather | solution.py:107
  35.6 340.2 %all-gather.13.cloned.1.call-start = ((), (), s32[]{:S(2)}) async-start(), calls=%async_computation.4 | async-start | bytes 1622016 | tf_op jit(solution)/shard_map/all_gather | solution.py:108
  201.0 174.8 %copy-start.3 = (f32[256,2,64]{2,1,0:T(2,128)}, f32[256,2,64]{2,1,0:T(2,128)S(1)}, u32[]{:S(2)}) copy-start(f32[256,2,64]{2,1,0:T(2,128)S(1)} %all-gather.2) | copy-start | bytes 393220
  282.0 89.3 %copy-start.4 = (f32[64,4,2]{1,2,0:T(2,128)}, f32[64,4,2]{1,2,0:T(2,128)S(1)}, u32[]{:S(2)}) copy-start(f32[64,4,2]{1,2,0:T(2,128)S(1)} %all-gather.4) | copy-start | bytes 6148
  370.0 1.3 copy-start.5
  371.3 4.5 copy-start.1
  384.0 15.0 %slice-start = ((f32[256,2,64]{2,1,0:T(2,128)}), f32[4,2,64]{2,1,0:T(2,128)S(1)}, s32[]{:S(2)}) async-start(f32[256,2,64]{2,1,0:T(2,128)} %copy-done.3), calls=%async_computation.5 | async-start | bytes 8192 | tf_op jit(solution)/shard_map/slice | solution.py:15
  384.0 15.0 %slice-start.1 = ((f32[64,4,2]{1,2,0:T(2,128)}), f32[63,4,2]{1,2,0:T(2,128)S(1)}, s32[]{:S(2)}) async-start(f32[64,4,2]{1,2,0:T(2,128)} %copy-done.4), calls=%async_computation.6 | async-start | bytes 129024 | tf_op jit(solution)/shard_map/slice | solution.py:16
  384.0 15.0 %slice-start.2 = ((f32[64,4,2]{1,2,0:T(2,128)}), f32[63,4,2]{1,2,0:T(2,128)S(1)}, s32[]{:S(2)}) async-start(f32[64,4,2]{1,2,0:T(2,128)} %copy-done.5), calls=%async_computation.7 | async-start | bytes 129024 | tf_op jit(solution)/shard_map/slice | solution.py:16
  384.0 34.0 %copy-start.12 = (bf16[4,128]{1,0:T(4,128)(2,1)S(1)}, bf16[4,128]{1,0:T(4,128)(2,1)}, u32[]{:S(2)}) copy-start(bf16[4,128]{1,0:T(4,128)(2,1)} %param.22) | copy-start | bytes 3076
  384.0 34.0 %copy-start.13 = (bf16[4,128]{1,0:T(4,128)(2,1)S(1)}, bf16[4,128]{1,0:T(4,128)(2,1)}, u32[]{:S(2)}) copy-start(bf16[4,128]{1,0:T(4,128)(2,1)} %param.23) | copy-start | bytes 3076
  384.0 34.6 %copy-start.9 = (s32[64,2]{0,1:T(2,128)S(1)}, s32[64,2]{0,1:T(2,128)}, u32[]{:S(2)}) copy-start(s32[64,2]{0,1:T(2,128)} %param.32) | copy-start | bytes 1540
  384.0 34.7 %copy-start.14 = (f32[64,2]{0,1:T(2,128)S(1)}, f32[64,2]{0,1:T(2,128)}, u32[]{:S(2)}) copy-start(f32[64,2]{0,1:T(2,128)} %param.33) | copy-start | bytes 1540
  384.0 56.6 %copy-start.18 = (s32[128]{0:T(128)S(1)}, s32[128]{0:T(128)}, u32[]{:S(2)}) copy-start(s32[128]{0:T(128)} %copy-done.17) | copy-start | bytes 1540
  384.1 56.6 %copy-start.15 = (f32[4,2]{0,1:T(2,128)S(1)}, f32[4,2]{0,1:T(2,128)}, u32[]{:S(2)}) copy-start(f32[4,2]{0,1:T(2,128)} %param.35) | copy-start | bytes 100
  384.1 56.6 %copy-start.16 = (s32[4,2]{0,1:T(2,128)S(1)}, s32[4,2]{0,1:T(2,128)}, u32[]{:S(2)}) copy-start(s32[4,2]{0,1:T(2,128)} %param.34) | copy-start | bytes 100
  384.1 56.6 %copy-start.10 = (bf16[4,1024]{1,0:T(4,128)(2,1)S(1)}, bf16[4,1024]{1,0:T(4,128)(2,1)}, u32[]{:S(2)}) copy-start(bf16[4,1024]{1,0:T(4,128)(2,1)} %param.30) | copy-start | bytes 24580
  384.1 56.7 %copy-start.8 = (f32[1024]{0:T(1024)S(1)}, f32[1024]{0:T(1024)}, u32[]{:S(2)}) copy-start(f32[1024]{0:T(1024)} %param.36) | copy-start | bytes 12292
  384.1 341.0 %all-to-all-start.1 = ((bf16[64,10,1024]{2,1,0:T(8,128)(2,1)}), bf16[64,10,1024]{2,1,0:T(8,128)(2,1)S(1)}, u32[]{:S(2)}, u32[]{:S(2)}) async-start(bf16[64,10,1024]{2,1,0:T(8,128)(2,1)} %reshape.154), calls=%async_computation.1 | async-start | bytes 4194304 | tf_op jit(solution)/shard_map/all_to_all | solution.py:166
  726.4 1.1 copy-start.2
Sparse Core Ops, SparseCore 0:
  10.1 36.1 all-gather.8
  48.5 33.4 all-gather.10
  84.0 33.4 all-gather.12
where the time goes:
time: 735 us
  blocking collectives  632 us (86%)
  starting transfers between devices  33.7 us (5%)
  local copies, waits for them, and re-layouts  23.1 us (3%)
  matrix products  16.3 us (2%)
  between operations  14.2 us (2%)
  other arithmetic  12.9 us (2%)
    all_gather x3, blocking collectives, combined_all(): pieces = jax.tree.map(lambda part: lax.all_gather(part, axis), value)  332 us
    psum x1, blocking collectives, body(): dec_terms = lax.psum(gate_here[:, None] * dec_part, 'seq')  279 us
    psum x1, blocking collectives, body(): attended = lax.psum(head_terms, 'tp')  21.6 us
    all_to_all x1, starting transfers between devices, body(): lax.all_to_all(send_all, 'seq', split_axis=0, concat_axis=0, tiled=True)  18.7 us
    all_to_all x1, starting transfers between devices, body(): lax.all_to_all(expert_apply(lax.all_to_all(send_all, 'seq', split_axis=0,...  14.8 us
  transfers between devices with their start and end apart: 5, of which 0 were waited for; matrix products, arithmetic and copies ran while one was open for 5% of the time, Pallas kernels for 0%

commit v1 on v0

--- a/solution.py
+++ b/solution.py
@@ -160,7 +160,7 @@
     my_expert = seq_index // shards
     dec_part = expert_block(normed_dec, weights).astype(jnp.float32)
     gate_here = jnp.sum(jnp.where(dec_routes == my_expert, dec_gates, 0.0), axis=1)
-    dec_terms = lax.psum(gate_here[:, None] * dec_part, "seq")
+    dec_terms = jnp.sum(lax.all_gather(gate_here[:, None] * dec_part, "seq"), axis=0)
     decode_out = (decode_hidden.astype(jnp.float32) + dec_terms).astype(jnp.bfloat16)
     send_all, index_all = pack_rows(normed_pre, routes, CAP, shards)
     back_all = lax.all_to_all(

time: 735 us -> 599 us (0.81)
  blocking collectives: 632 us -> 353 us
  waiting for transfers between devices: 2.08 us -> 142 us
    psum x1 -> x0, blocking collectives: 279 us -> none  [body(): dec_terms = lax.psum(gate_here[:, None] * dec_part, 'seq')]
    all_gather x0 -> x1, waiting for transfers between devices: none -> 140 us  [body(): lax.all_gather(gate_here[:, None] * dec_part, 'seq')]
  transfers between devices with their start and end apart: 5 -> 6, of which waited for: 0 -> 1; matrix products, arithmetic and copies ran while one was open for 5% -> 7% of each run, Pallas kernels for 0% -> 0%
where the time goes in v1:
time: 599 us; the launch traced here: 598 us
  blocking collectives  353 us (59%)
  waiting for transfers between devices  142 us (24%)
  starting transfers between devices  34 us (6%)
  local copies, waits for them, and re-layouts  22.9 us (4%)
  matrix products  16.9 us (3%)
  other arithmetic  14.3 us (2%)
  between operations  14.2 us (2%)
    all_gather x3, blocking collectives, combined_all(): pieces = jax.tree.map(lambda part: lax.all_gather(part, axis), value)  331 us
    all_gather x1, waiting for transfers between devices, body(): lax.all_gather(gate_here[:, None] * dec_part, 'seq')  140 us
    psum x1, blocking collectives, body(): attended = lax.psum(head_terms, 'tp')  21.6 us
    all_to_all x1, starting transfers between devices, body(): lax.all_to_all(send_all, 'seq', split_axis=0, concat_axis=0, tiled=True)  18.7 us
    all_to_all x1, starting transfers between devices, body(): lax.all_to_all(expert_apply(lax.all_to_all(send_all, 'seq', split_axis=0,...  15.2 us
  transfers between devices with their start and end apart: 6, of which 1 were waited for; matrix products, arithmetic and copies ran while one was open for 7% of the time, Pallas kernels for 0%

profile of v1, /device:TPU:8, one launch (start us, length us, event | category | flops | bytes accessed | tf_op | source)
XLA Modules:
  0.0 598.0 jit_solution(11617097017761749064)
XLA Ops:
  7.2 0.7 all-gather.12.cloned.1.call-update
  7.9 0.8 copy.57
  8.7 0.1 reshape.149
  8.8 0.7 broadcast_multiply_fusion
  9.6 0.1 mul.213
  9.7 1.0 fusion.18
  10.8 1.0 fusion.20
  11.8 0.1 broadcast_in_dim.66
  12.2 0.2 reduce_window_sum.11
  12.3 0.2 select_reduce_fusion
  12.5 0.5 copy-done.17
  13.0 1.2 scatter_custom_fusion
  14.2 0.1 reshape.151
  14.4 1.6 broadcast_in_dim.67
  16.0 18.7 %all-to-all-start = ((bf16[64,10,1024]{2,1,0:T(8,128)(2,1)}), bf16[64,10,1024]{2,1,0:T(8,128)(2,1)S(1)}, u32[]{:S(2)}, u32[]{:S(2)}) async-start(bf16[64,10,1024]{2,1,0:T(8,128)(2,1)} %bitcast.20), calls=%async_computation | async-start | bytes 4194304 | tf_op jit(solution)/shard_map/all_to_all | solution.py:168
  34.8 0.7 all-gather.14.cloned.1.call-update
  35.5 0.7 all-gather.16.cloned.1.call-update
  36.2 0.1 copy.67
  36.6 0.7 constant_dynamic-slice_fusion.1
  37.3 0.1 fusion.67
  37.5 0.2 fusion.66
  37.7 0.2 fusion.65
  37.9 0.2 fusion.24
  38.1 162.8 %all-gather.2 = f32[256,2,64]{2,1,0:T(2,128)S(1)} all-gather(f32[4,2,64]{2,1,0:T(2,128)S(1)} %bitcast.72), channel_id=4, replica_groups=mesh['seq'=64,'tp'=8] {'seq'}, dimensions={0}, use_global_device_ids=true | all-gather | bytes 133120 | tf_op jit(solution)/shard_map/all_gather | solution.py:14
  201.1 80.8 %all-gather.5 = f32[64,4,2]{1,2,0:T(2,128)S(1)} all-gather(f32[1,4,2]{1,2,0:T(2,128)S(1)} %bitcast.74), channel_id=3, replica_groups=mesh['seq'=64,'tp'=8] {'seq'}, dimensions={0}, use_global_device_ids=true | all-gather | bytes 2080 | tf_op jit(solution)/shard_map/all_gather | solution.py:14
  281.9 87.9 %all-gather.4 = f32[64,4,2]{1,2,0:T(2,128)S(1)} all-gather(f32[1,4,2]{1,2,0:T(2,128)S(1)} %bitcast.73), channel_id=2, replica_groups=mesh['seq'=64,'tp'=8] {'seq'}, dimensions={0}, use_global_device_ids=true | all-gather | bytes 2080 | tf_op jit(solution)/shard_map/all_gather | solution.py:14
  369.7 1.3 reshape.153
  371.1 4.4 fusion.69
  375.5 6.6 %convolution_convert_fusion = bf16[640,1024]{1,0:T(8,128)(2,1)S(1)} fusion(bf16[704,1024]{1,0:T(8,128)(2,1)} %all-gather.16.cloned.1.call-done, f32[640,704]{0,1:T(8,128)} %fusion.69, bf16[640,1024]{1,0:T(8,128)(2,1)S(1)} %copy-done.1, bf16[1024,704]{0,1:T(8,128)(2,1)} %all-gather.14.cloned.1.call-done), kind=kOutput, calls=%fused_computation.22 | convolution fusion | flops 1850654720 | bytes 7307264 | tf_op jit(solution)/shard_map/dot_general | solution.py:62
  382.1 1.6 reshape.154
  383.8 15.2 %all-to-all-start.1 = ((bf16[64,10,1024]{2,1,0:T(8,128)(2,1)}), bf16[64,10,1024]{2,1,0:T(8,128)(2,1)S(1)}, u32[]{:S(2)}, u32[]{:S(2)}) async-start(bf16[64,10,1024]{2,1,0:T(8,128)(2,1)} %reshape.154), calls=%async_computation.1 | async-start | bytes 4194304 | tf_op jit(solution)/shard_map/all_to_all | solution.py:166
  399.0 18.6 %while.14 = (s32[]{:T(128)}, f32[4,2]{0,1:T(2,128)S(1)}, f32[4,2]{0,1:T(2,128)S(1)}, f32[4,2,64]{2,1,0:T(2,128)S(1)}, f32[63,4,2]{1,2,0:T(2,128)S(1)}, /*index=5...) while((s32[]{:T(128)}, f32[4,2]{0,1:T(2,128)S(1)}, f32[4,2]{0,1:T(2,128)S(1)}, ...), condition=%wide.region_3.4_spmd, body=%wide.region_2.3_spmd.sunk | while | flops 1586 | bytes 6685 | solution.py:17
  418.0 0.1 slice_reduce_fusion
  418.5 0.1 fusion.68
  418.6 21.6 %psum.7 = f32[4,1024]{1,0:T(4,128)S(1)} all-reduce(f32[4,1024]{1,0:T(4,128)S(1)} %fusion.68), channel_id=1, replica_groups=mesh['seq'=64,'tp'=8] {'tp'}, use_global_device_ids=true, to_apply=%region_5.6 | all-reduce | flops 4096 | bytes 32768 | tf_op jit(solution)/shard_map/psum | solution.py:157
  440.2 0.1 fusion.28
  440.4 1.8 fusion.60
  442.2 3.3 fusion.14
  445.6 0.1 reduce_sum.91
  445.8 0.1 copy.59
  446.1 140.3 %all-gather.18.cloned.1.call-done = f32[64,4,1024]{2,1,0:T(4,128)} async-done(((f32[1,4,1024]{2,1,0:T(4,128)}), f32[64,4,1024]{2,1,0:T(4,128)}) %all-gather.18.cloned.1.call-update) | async-done | bytes 1048592 | tf_op jit(solution)/shard_map/all_gather | solution.py:163
  586.3 1.4 reduce_sum.89
  587.7 0.6 fusion.31
  588.4 0.4 convert_reduce_fusion
  588.9 0.8 gather_fusion
  589.7 0.3 gather.7
  590.0 0.8 multiply_reduce_fusion
  590.8 0.7 fusion.21
  (339 shorter events, 20.4 us)
Async XLA Ops:
  7.2 411.3 %copy-start = (bf16[128,1024]{1,0:T(8,128)(2,1)S(1)}, bf16[128,1024]{1,0:T(8,128)(2,1)}, u32[]{:S(2)}) copy-start(bf16[128,1024]{1,0:T(8,128)(2,1)} %param.29) | copy-start | bytes 786436
  7.2 363.9 %all-gather.12.cloned.1.call-start = ((), (), s32[]{:S(2)}) async-start(), calls=%async_computation.2 | async-start | bytes 1622016 | tf_op jit(solution)/shard_map/all_gather | solution.py:106
  12.5 0.5 copy-start.17
  16.0 20.2 %copy-start.6 = (bf16[4,64,128]{2,1,0:T(8,128)(2,1)S(1)}, bf16[4,64,128]{2,1,0:T(8,128)(2,1)}, u32[]{:S(2)}) copy-start(bf16[4,64,128]{2,1,0:T(8,128)(2,1)} %param.24) | copy-start | bytes 196612
  16.0 20.4 %copy-start.11 = (bf16[4,128]{1,0:T(4,128)(2,1)S(1)}, bf16[4,128]{1,0:T(4,128)(2,1)}, u32[]{:S(2)}) copy-start(bf16[4,128]{1,0:T(4,128)(2,1)} %param.21) | copy-start | bytes 3076
  16.0 20.5 %copy-start.7 = (bf16[4,64,128]{2,1,0:T(8,128)(2,1)S(1)}, bf16[4,64,128]{2,1,0:T(8,128)(2,1)}, u32[]{:S(2)}) copy-start(bf16[4,64,128]{2,1,0:T(8,128)(2,1)} %param.25) | copy-start | bytes 196612
  16.0 21.3 %copy-start.20 = (s32[4]{0:T(128)S(1)}, s32[4]{0:T(128)}, u32[]{:S(2)}) copy-start(s32[4]{0:T(128)} %param.27) | copy-start | bytes 52
  16.0 21.5 %copy-start.19 = (s32[4,64]{1,0:T(4,128)S(1)}, s32[4,64]{1,0:T(4,128)}, u32[]{:S(2)}) copy-start(s32[4,64]{1,0:T(4,128)} %param.26) | copy-start | bytes 3076
  16.0 353.7 %all-to-all-start = ((bf16[64,10,1024]{2,1,0:T(8,128)(2,1)}), bf16[64,10,1024]{2,1,0:T(8,128)(2,1)S(1)}, u32[]{:S(2)}, u32[]{:S(2)}) async-start(bf16[64,10,1024]{2,1,0:T(8,128)(2,1)} %bitcast.20), calls=%async_computation | async-start | bytes 4194304 | tf_op jit(solution)/shard_map/all_to_all | solution.py:168
  34.7 340.8 %all-gather.14.cloned.1.call-start = ((), (), s32[]{:S(2)}) async-start(), calls=%async_computation.3 | async-start | bytes 1622016 | tf_op jit(solution)/shard_map/all_gather | solution.py:107
  35.5 340.1 %all-gather.16.cloned.1.call-start = ((), (), s32[]{:S(2)}) async-start(), calls=%async_computation.4 | async-start | bytes 1622016 | tf_op jit(solution)/shard_map/all_gather | solution.py:108
  200.9 174.7 %copy-start.3 = (f32[256,2,64]{2,1,0:T(2,128)}, f32[256,2,64]{2,1,0:T(2,128)S(1)}, u32[]{:S(2)}) copy-start(f32[256,2,64]{2,1,0:T(2,128)S(1)} %all-gather.2) | copy-start | bytes 393220
  281.9 89.2 %copy-start.4 = (f32[64,4,2]{1,2,0:T(2,128)}, f32[64,4,2]{1,2,0:T(2,128)S(1)}, u32[]{:S(2)}) copy-start(f32[64,4,2]{1,2,0:T(2,128)S(1)} %all-gather.5) | copy-start | bytes 6148
  369.7 1.3 copy-start.5
  371.1 4.4 copy-start.1
  383.7 15.3 %slice-start = ((f32[256,2,64]{2,1,0:T(2,128)}), f32[4,2,64]{2,1,0:T(2,128)S(1)}, s32[]{:S(2)}) async-start(f32[256,2,64]{2,1,0:T(2,128)} %copy-done.3), calls=%async_computation.6 | async-start | bytes 8192 | tf_op jit(solution)/shard_map/slice | solution.py:15
  383.7 15.3 %slice-start.1 = ((f32[64,4,2]{1,2,0:T(2,128)}), f32[63,4,2]{1,2,0:T(2,128)S(1)}, s32[]{:S(2)}) async-start(f32[64,4,2]{1,2,0:T(2,128)} %copy-done.4), calls=%async_computation.7 | async-start | bytes 129024 | tf_op jit(solution)/shard_map/slice | solution.py:16
  383.7 15.3 %slice-start.2 = ((f32[64,4,2]{1,2,0:T(2,128)}), f32[63,4,2]{1,2,0:T(2,128)S(1)}, s32[]{:S(2)}) async-start(f32[64,4,2]{1,2,0:T(2,128)} %copy-done.5), calls=%async_computation.8 | async-start | bytes 129024 | tf_op jit(solution)/shard_map/slice | solution.py:16
  383.7 34.2 %copy-start.12 = (bf16[4,128]{1,0:T(4,128)(2,1)S(1)}, bf16[4,128]{1,0:T(4,128)(2,1)}, u32[]{:S(2)}) copy-start(bf16[4,128]{1,0:T(4,128)(2,1)} %param.22) | copy-start | bytes 3076
  383.7 34.2 %copy-start.13 = (bf16[4,128]{1,0:T(4,128)(2,1)S(1)}, bf16[4,128]{1,0:T(4,128)(2,1)}, u32[]{:S(2)}) copy-start(bf16[4,128]{1,0:T(4,128)(2,1)} %param.23) | copy-start | bytes 3076
  383.7 56.5 %copy-start.14 = (f32[4,2]{0,1:T(2,128)S(1)}, f32[4,2]{0,1:T(2,128)}, u32[]{:S(2)}) copy-start(f32[4,2]{0,1:T(2,128)} %param.35) | copy-start | bytes 100
  383.7 56.5 %copy-start.15 = (s32[4,2]{0,1:T(2,128)S(1)}, s32[4,2]{0,1:T(2,128)}, u32[]{:S(2)}) copy-start(s32[4,2]{0,1:T(2,128)} %param.34) | copy-start | bytes 100
  383.7 56.5 %copy-start.10 = (bf16[4,1024]{1,0:T(4,128)(2,1)S(1)}, bf16[4,1024]{1,0:T(4,128)(2,1)}, u32[]{:S(2)}) copy-start(bf16[4,1024]{1,0:T(4,128)(2,1)} %param.30) | copy-start | bytes 24580
  383.8 56.6 %copy-start.8 = (f32[1024]{0:T(1024)S(1)}, f32[1024]{0:T(1024)}, u32[]{:S(2)}) copy-start(f32[1024]{0:T(1024)} %param.36) | copy-start | bytes 12292
  383.8 204.6 %all-to-all-start.1 = ((bf16[64,10,1024]{2,1,0:T(8,128)(2,1)}), bf16[64,10,1024]{2,1,0:T(8,128)(2,1)S(1)}, u32[]{:S(2)}, u32[]{:S(2)}) async-start(bf16[64,10,1024]{2,1,0:T(8,128)(2,1)} %reshape.154), calls=%async_computation.1 | async-start | bytes 4194304 | tf_op jit(solution)/shard_map/all_to_all | solution.py:166
  398.9 187.4 %all-gather.18.cloned.1.call-start = ((), (), s32[]{:S(2)}) async-start(), calls=%async_computation.5 | async-start | bytes 1064960 | tf_op jit(solution)/shard_map/all_gather | solution.py:163
  442.2 3.6 copy-start.9
  442.2 3.7 copy-start.16
  442.2 3.8 copy-start.18
  589.7 1.1 copy-start.2
Sparse Core Ops, SparseCore 0:
  10.1 36.1 all-gather.11
  48.5 33.4 all-gather.13
  84.0 33.4 all-gather.15
  445.7 140.5 all-gather.17
